TPU v7x, 32 devices: a whole 2x2x4 slice. The times are simulated.
32 devices in a mesh: inner: 8 (over z, y), cols: 4 (over x, core).
Axes of the slice: x: 2, y: 2, z: 4, core: 2. Of those that a mesh axis runs over, the one named last changes fastest.
Arguments:
- left_u: bfloat16 [64, 512, 128], P(('inner', 'cols')), may hold values from -6 to 6
- left_v: bfloat16 [64, 512, 128], P(('inner', 'cols')), may hold values from -0.0234375 to 0.0234375
- right_u: bfloat16 [16, 64, 512, 128], P('cols', 'inner'), may hold values from -6 to 6
- right_v: bfloat16 [16, 64, 512, 128], P('cols', 'inner'), may hold values from -0.1875 to 0.1875
- sketch: bfloat16 [16, 512, 128], P('cols'), may hold values from -0.25 to 0.25
- tile_index: int32 [16, 64], P('cols', 'inner'), may hold values from 0 to 63, as said below
- slot_mask: int32 [16, 64], P('cols', 'inner'), may hold values from 0 to 1, as said below
Outputs:
- basis: float32 [16, 512, 128], P('cols', 'inner')
- coeff: float32 [16, 512, 128], P('cols', 'inner')
Inputs may be any that keep to these rules, and one draw needn't show every extreme that they name: `tile_index`: slot s of an output tile belongs to inner group g = s // 8 and names a left tile of that group, g * 8 to g * 8 + 7; the tiles named by one output tile's slots of one group are distinct. `slot_mask`: in each output tile and inner group the live slots come first and there is at least one; in every output tile some group has all 8 slots live, and the others at most 4.
All inputs are finite; a program needn't handle non-finite values.
Results may differ from a plain program's by a relative error of at most 0.0045.
Values may be sent and summed in bfloat16 or wider, within the bound.
A program may use at most 64 MiB of HBM per device.

v0:
```python
import math
import jax
import jax.numpy as jnp
from jax import lax
from jax.sharding import PartitionSpec as P

NB = 512
HIGH = lax.Precision.HIGHEST


def orthonormal(sketch_rows, factor):
    solved = jax.scipy.linalg.solve_triangular(factor, jnp.swapaxes(sketch_rows, 1, 2), lower=True)
    return jnp.swapaxes(solved, 1, 2)


def gram_of(sketch_rows):
    return jnp.einsum("ona,onb->oab", sketch_rows, sketch_rows, precision=HIGH)


def body(left_u, left_v, right_u, right_v, sketch, tile_index, slot_mask):
    group_u, group_v = (
        lax.all_gather(left_u, "cols", axis=0, tiled=True),
        lax.all_gather(left_v, "cols", axis=0, tiled=True),
    )
    group_tiles = group_u.shape[0]
    local_idx = tile_index - lax.axis_index("inner") * group_tiles
    live_mask = slot_mask.astype(jnp.float32)[..., None, None]
    tile_u = jnp.take(group_u, local_idx, axis=0)
    tile_v = jnp.take(group_v, local_idx, axis=0)
    pairing = jnp.einsum("osna,osnb->osab", tile_v, right_u, preferred_element_type=jnp.float32)
    probes = jnp.einsum("osnb,ont->osbt", right_v, sketch, preferred_element_type=jnp.float32)
    mixing = (live_mask * jnp.einsum("osab,osbt->osat", pairing, probes, precision=HIGH)).astype(
        jnp.bfloat16
    )
    partial_sketch = jnp.einsum(
        "osna,osat->ont", tile_u, mixing, preferred_element_type=jnp.float32
    )
    scale_up = math.sqrt(NB)
    summed = lax.psum(partial_sketch, "inner")
    factor = jnp.linalg.cholesky(gram_of(summed))
    ortho = orthonormal(summed, factor)
    row_count = summed.shape[1] // lax.axis_size("inner")
    row_start = lax.axis_index("inner") * row_count
    basis = lax.dynamic_slice_in_dim(ortho, row_start, row_count, 1) * scale_up
    full_basis = ortho.astype(jnp.bfloat16)
    projected = jnp.einsum("osna,ont->osat", tile_u, full_basis, preferred_element_type=jnp.float32)
    backward = (
        live_mask * jnp.einsum("osab,osat->osbt", pairing, projected, precision=HIGH)
    ).astype(jnp.bfloat16)
    coeff_terms = jnp.einsum(
        "osnb,osbt->ont", right_v, backward, preferred_element_type=jnp.float32
    )
    coeff = lax.psum_scatter(coeff_terms, "inner", scatter_dimension=1, tiled=True)
    return (basis, coeff)


def solution(mesh):
    return jax.shard_map(
        body,
        mesh=mesh,
        in_specs=(
            P(("inner", "cols"), None, None),
            P(("inner", "cols"), None, None),
            P("cols", "inner", None, None),
            P("cols", "inner", None, None),
            P("cols", None, None),
            P("cols", "inner"),
            P("cols", "inner"),
        ),
        out_specs=(P("cols", "inner", None), P("cols", "inner", None)),
        check_vma=False,
    )
```

profile of v0, /device:TPU:0, one launch (start us, length us, event | category | flops | bytes accessed | tf_op | source)
XLA Modules:
  0.0 335.3 jit_solution(5929237776262730713)
XLA Ops:
  7.2 0.0 copy-start
  7.2 0.0 all-gather.5.cloned.1.call-start
  7.2 0.7 all-gather.5.cloned.1.call-update
  7.9 0.0 all-gather.3.cloned.1.call-start
  8.0 0.7 all-gather.3.cloned.1.call-update
  8.7 0.0 all-reduce.4.cloned.1.call-start
  8.7 0.7 compare_and_fusion
  9.4 0.1 reshape.41
  9.5 0.7 convert_element_type.12
  10.2 0.0 copy-done
  10.2 3.8 %fusion.10 = f32[4,8,128,128]{3,2,1,0:T(8,128)S(1)} fusion(bf16[4,8,512,128]{3,2,1,0:T(8,128)(2,1)} %param.12, bf16[4,512,128]{2,1,0:T(8,128)(2,1)S(1)} %copy-done), kind=kOutput, calls=%fused_computation.16 | convolution fusion | flops 536870912 | bytes 6815744 | tf_op jit(solution)/shard_map/osnb,ont->osbt/dot_general | solution.py:31
  14.0 15.0 %all-gather.5.cloned.1.call-done = bf16[8,512,128]{2,1,0:T(8,128)(2,1)} async-done(((bf16[2,512,128]{2,1,0:T(8,128)(2,1)}), bf16[8,512,128]{2,1,0:T(8,128)(2,1)}) %all-gather.5.cloned.1.call-update) | async-done | bytes 1048592 | tf_op jit(solution)/shard_map/all_gather | solution.py:23
  29.0 4.3 %gather_fusion.1 = bf16[32,512,128]{2,1,0:T(8,128)(2,1)} fusion(bf16[8,512,128]{2,1,0:T(8,128)(2,1)} %all-gather.5.cloned.1.call-done, s32[1024]{0:T(1024)S(1)} %pad_clamp_fusion), kind=kCustom, calls=%fused_computation.1.clone | custom fusion | bytes 8388736 | tf_op jit(solution)/shard_map/jit(_take)/gather | solution.py:29
  33.3 6.3 %copy.23 = bf16[4,8,512,128]{2,3,1,0:T(8,128)(2,1)} copy(bf16[4,8,512,128]{3,2,1,0:T(8,128)(2,1)} %bitcast.43) | data formatting | bytes 8388608 | tf_op jit(solution)/shard_map/jit(_take)/gather | solution.py:29
  39.6 7.7 %all-gather.3.cloned.1.call-done = bf16[8,512,128]{2,1,0:T(8,128)(2,1)} async-done(((bf16[2,512,128]{2,1,0:T(8,128)(2,1)}), bf16[8,512,128]{2,1,0:T(8,128)(2,1)}) %all-gather.3.cloned.1.call-update) | async-done | bytes 1048592 | tf_op jit(solution)/shard_map/all_gather | solution.py:22
  47.3 4.3 %gather_fusion = bf16[32,512,128]{2,1,0:T(8,128)(2,1)} fusion(bf16[8,512,128]{2,1,0:T(8,128)(2,1)} %all-gather.3.cloned.1.call-done, s32[1024]{0:T(1024)S(1)} %pad_clamp_fusion), kind=kCustom, calls=%fused_computation.clone | custom fusion | bytes 8388736 | tf_op jit(solution)/shard_map/jit(_take)/gather | solution.py:28
  51.6 6.2 %copy.22 = bf16[4,8,512,128]{2,3,1,0:T(8,128)(2,1)} copy(bf16[4,8,512,128]{3,2,1,0:T(8,128)(2,1)} %bitcast.42) | data formatting | bytes 8388608 | tf_op jit(solution)/shard_map/jit(_take)/gather | solution.py:28
  57.7 4.8 %fusion = f32[4,8,128,128]{3,2,1,0:T(8,128)S(1)} fusion(bf16[4,8,512,128]{3,2,1,0:T(8,128)(2,1)} %param.11, bf16[4,8,512,128]{2,3,1,0:T(8,128)(2,1)} %copy.23, pred[4,8]{1,0:T(4,128)(4,1)S(1)} %get-tuple-element.9), kind=kOutput, calls=%fused_computation.2 | convolution fusion | flops 538968064 | bytes 10485792 | tf_op jit(solution)/shard_map/osna,osnb->osab/dot_general | solution.py:30
  62.5 0.0 copy-start.3
  62.6 1.3 copy-done.3
  63.9 0.0 copy-start.5
  63.9 2.3 multiply_convert_fusion.1
  66.2 0.0 copy-done.5
  66.2 2.8 fusion.8
  69.0 0.0 all-reduce.4.cloned.1.call-update
  69.0 0.2 all-reduce.6.cloned.1.call-start
  69.3 78.1 %all-reduce.4.cloned.1.call-done = f32[4,512,128]{2,1,0:T(8,128)} async-done(((f32[4,512,128]{2,1,0:T(8,128)}), f32[4,512,128]{2,1,0:T(8,128)}) %all-reduce.4.cloned.1.call-update) | async-done | bytes 1048592 | tf_op jit(solution)/shard_map/psum | solution.py:39
  147.4 0.0 copy-start.2
  147.4 3.4 %fusion.19 = f32[4,128,128]{2,1,0:T(8,128)S(1)} fusion(f32[4,512,128]{2,1,0:T(8,128)} %all-reduce.4.cloned.1.call-done), kind=kOutput, calls=%fused_computation.36 | convolution fusion | flops 402653184 | bytes 1310720 | tf_op jit(solution)/shard_map/ona,onb->oab/dot_general | solution.py:17
  150.8 0.1 copy.27
  151.0 46.9 %custom-call.8 = f32[4,128,128]{2,1,0:T(8,128)S(1)} custom-call(f32[4,128,128]{2,1,0:T(8,128)S(1)} %fusion.15), custom_call_target="Cholesky" | custom-call | tf_op jit(solution)/shard_map/jit(cholesky)/cholesky | solution.py:40
  198.0 0.1 compare_reduce_fusion
  198.1 0.1 select_bitcast_fusion
  198.2 39.5 %custom-call.9 = f32[4,1,128,128]{2,3,1,0:T(8,128)S(1)} custom-call(f32[4,1,128,128]{3,2,1,0:T(8,128)S(1)} %select_bitcast_fusion), custom_call_target="InvertDiagBlocksLowerTriangular" | custom-call | tf_op jit(solution)/shard_map/jit(_solve_triangular)/vmap()/triangular_solve | solution.py:12
  237.7 0.0 copy-done.2
  237.7 1.0 fusion.13
  238.8 0.0 copy-start.4
  238.8 3.6 %fusion.3 = f32[4,8,128,128]{3,2,1,0:T(8,128)S(1)} fusion(bf16[4,8,512,128]{2,3,1,0:T(8,128)(2,1)} %copy.22, pred[4,8]{1,0:T(4,128)(4,1)S(1)} %get-tuple-element.9, f32[4,512,128]{2,1,0:T(8,128)S(1)} %fusion.13), kind=kOutput, calls=%fused_computation.6 | convolution fusion | flops 539230208 | bytes 7340064 | tf_op jit(solution)/shard_map/osna,ont->osat/dot_general | solution.py:46
  242.4 0.0 copy-done.4
  242.4 0.0 copy-start.1
  242.5 3.7 %multiply_convert_fusion = bf16[4,8,128,128]{3,2,1,0:T(8,128)(2,1)S(1)} fusion(f32[4,8,128,128]{3,2,1,0:T(8,128)S(1)} %copy-done.4, f32[4,8,128,128]{3,2,1,0:T(8,128)S(1)} %fusion.3, f32[4,8]{1,0:T(4,128)S(1)} %convert_element_type.12), kind=kOutput, calls=%fused_computation.11 | convolution fusion | flops 806354944 | bytes 5243008 | tf_op jit(solution)/shard_map/osab,osat->osbt/dot_general | solution.py:48
  246.2 0.0 copy-done.1
  246.2 0.0 copy-start.6
  246.2 1.5 convolution_bitcast_fusion
  247.7 1.4 copy.31
  249.1 0.0 all-reduce.6.cloned.1.call-update
  249.1 0.0 copy-done.6
  249.2 0.6 dynamic-slice
  250.4 0.7 dynamic-slice_multiply_fusion
  251.1 76.1 %all-reduce.6.cloned.1.call-done = f32[4,512,128]{2,0,1:T(4,128)} async-done(((f32[4,512,128]{2,0,1:T(4,128)}), f32[4,512,128]{2,0,1:T(4,128)}) %all-reduce.6.cloned.1.call-update) | async-done | bytes 1048592
  327.2 0.9 constant_dynamic-slice_fusion
  328.1 0.7 copy.32
  (5 shorter events, 0.1 us)
Async XLA Ops:
  7.2 3.0 copy-start
  7.2 21.8 %all-gather.5.cloned.1.call-start = ((), (), s32[]{:S(2)}) async-start(), calls=%async_computation.1 | async-start | bytes 1310720 | tf_op jit(solution)/shard_map/all_gather | solution.py:23
  7.9 39.4 %all-gather.3.cloned.1.call-start = ((), (), s32[]{:S(2)}) async-start(), calls=%async_computation | async-start | bytes 1310720 | tf_op jit(solution)/shard_map/all_gather | solution.py:22
  8.7 138.7 %all-reduce.4.cloned.1.call-start = ((), (), s32[]{:S(2)}) async-start(), calls=%async_computation.2 | async-start | bytes 2097152 | tf_op jit(solution)/shard_map/psum | solution.py:39
  62.5 1.3 copy-start.3
  63.9 2.3 copy-start.5
  69.0 258.2 %all-reduce.6.cloned.1.call-start = ((), (), s32[]{:S(2)}) async-start(), calls=%async_computation.3 | async-start | bytes 2097152
  147.4 90.3 %copy-start.2 = (f32[4,512,128]{2,1,0:T(8,128)S(1)}, f32[4,512,128]{2,1,0:T(8,128)}, u32[]{:S(2)}) copy-start(f32[4,512,128]{2,1,0:T(8,128)} %all-reduce.4.cloned.1.call-done) | copy-start | bytes 3145732
  238.8 3.7 %copy-start.4 = (f32[4,8,128,128]{3,2,1,0:T(8,128)S(1)}, f32[4,8,128,128]{3,2,1,0:T(8,128)}, u32[]{:S(2)}) copy-start(f32[4,8,128,128]{3,2,1,0:T(8,128)} %copy-done.3) | copy-start | bytes 6291460
  242.4 3.8 %copy-start.1 = (bf16[4,8,512,128]{3,2,1,0:T(8,128)(2,1)S(1)}, bf16[4,8,512,128]{3,2,1,0:T(8,128)(2,1)}, u32[]{:S(2)}) copy-start(bf16[4,8,512,128]{3,2,1,0:T(8,128)(2,1)} %param.12) | copy-start | bytes 12582916
  246.2 2.9 copy-start.6
Sparse Core Ops, SparseCore 0:
  9.5 19.4 all-gather.4
  30.6 16.6 all-gather.2
  69.1 78.2 all-reduce.3
  249.3 77.8 all-reduce.5
where the time goes:
time: 336 us; the launch traced here: 335 us
  waiting for transfers between devices  178 us (53%)
  other arithmetic  88.8 us (26%)
  matrix products  27 us (8%)
  local copies, waits for them, and re-layouts  26.1 us (8%)
  between operations  14.6 us (4%)
    psum x1, waiting for transfers between devices, body(): summed = lax.psum(partial_sketch, 'inner')  78.1 us
    unnamed x5, waiting for transfers between devices  77.5 us
    another operation x4, other arithmetic, body(): factor = jnp.linalg.cholesky(gram_of(summed))  47.1 us
    another operation x3, other arithmetic, orthonormal(): jax.scipy.linalg.solve_triangular(factor, jnp.swapaxes(sketch_rows, 1, 2)...  39.7 us
    all_gather x1, waiting for transfers between devices, body(): lax.all_gather(left_v, 'cols', axis=0, tiled=True)  15 us
    gather x2, local copies, waits for them, and re-layouts, body(): tile_v = jnp.take(group_v, local_idx, axis=0)  10.6 us
    gather x2, local copies, waits for them, and re-layouts, body(): tile_u = jnp.take(group_u, local_idx, axis=0)  10.5 us
    all_gather x1, waiting for transfers between devices, body(): lax.all_gather(left_u, 'cols', axis=0, tiled=True)  7.72 us
  transfers between devices with their start and end apart: 4, of which 4 were waited for; matrix products, arithmetic and copies ran while one was open for 5% of the time, Pallas kernels for 0%

commit v1 on v0

--- a/solution.py
+++ b/solution.py
@@ -6,6 +6,19 @@
 
 NB = 512
 HIGH = lax.Precision.HIGHEST
+
+
+def remake_axis_part(xin):
+    ax_name = "inner"
+    n_shards = lax.axis_size(ax_name)
+    carry_out, z2 = (xin, 0)
+    while 1 << z2 < n_shards:
+        z = lax.ppermute(
+            carry_out, ax_name, perm=list(map(lambda to_i: (to_i, to_i ^ 1 << z2), range(n_shards)))
+        )
+        carry_out = carry_out + z
+        z2 = z2 + 1
+    return carry_out
 
 
 def orthonormal(sketch_rows, factor):
@@ -36,7 +49,7 @@
         "osna,osat->ont", tile_u, mixing, preferred_element_type=jnp.float32
     )
     scale_up = math.sqrt(NB)
-    summed = lax.psum(partial_sketch, "inner")
+    summed = remake_axis_part(partial_sketch)
     factor = jnp.linalg.cholesky(gram_of(summed))
     ortho = orthonormal(summed, factor)
     row_count = summed.shape[1] // lax.axis_size("inner")

time: 336 us -> 352 us (1.048)
  waiting for transfers between devices: 178 us -> 192 us
  starting transfers between devices: 0.34 us -> 5.68 us
    ppermute x0 -> x3, waiting for transfers between devices: none -> 91.2 us  [remake_axis_part(): lax.ppermute(carry_out, ax_name, perm=list(map(lambda to_i: (to_i, to_i ^...]
    psum x1 -> x0, waiting for transfers between devices: 78.1 us -> none  [body(): summed = lax.psum(partial_sketch, 'inner')]
    ppermute x0 -> x3, starting transfers between devices: none -> 5.57 us  [remake_axis_part(): lax.ppermute(carry_out, ax_name, perm=list(map(lambda to_i: (to_i, to_i ^...]
    unnamed x5 -> x4, waiting for transfers between devices: 77.5 us -> 77.9 us
  transfers between devices with their start and end apart: 4 -> 6, of which waited for: 4 -> 6; matrix products, arithmetic and copies ran while one was open for 5% -> 5% of each run, Pallas kernels for 0% -> 0%
where the time goes in v1:
time: 352 us; the launch traced here: 351 us
  waiting for transfers between devices  192 us (55%)
  other arithmetic  89.4 us (25%)
  local copies, waits for them, and re-layouts  25.6 us (7%)
  matrix products  24.4 us (7%)
  between operations  14.6 us (4%)
  starting transfers between devices  5.68 us (2%)
    ppermute x3, waiting for transfers between devices, remake_axis_part(): lax.ppermute(carry_out, ax_name, perm=list(map(lambda to_i: (to_i, to_i ^...  91.2 us
    unnamed x4, waiting for transfers between devices  77.9 us
    another operation x4, other arithmetic, body(): factor = jnp.linalg.cholesky(gram_of(summed))  47.3 us
    another operation x3, other arithmetic, orthonormal(): jax.scipy.linalg.solve_triangular(factor, jnp.swapaxes(sketch_rows, 1, 2)...  39.7 us
    all_gather x1, waiting for transfers between devices, body(): lax.all_gather(left_v, 'cols', axis=0, tiled=True)  15 us
    gather x2, local copies, waits for them, and re-layouts, body(): tile_v = jnp.take(group_v, local_idx, axis=0)  10.7 us
    gather x2, local copies, waits for them, and re-layouts, body(): tile_u = jnp.take(group_u, local_idx, axis=0)  10.5 us
    all_gather x1, waiting for transfers between devices, body(): lax.all_gather(left_u, 'cols', axis=0, tiled=True)  7.61 us
  transfers between devices with their start and end apart: 6, of which 6 were waited for; matrix products, arithmetic and copies ran while one was open for 5% of the time, Pallas kernels for 0%

profile of v1, /device:TPU:0, one launch (start us, length us, event | category | flops | bytes accessed | tf_op | source)
XLA Modules:
  0.0 351.5 jit_solution(3372208796655425218)
XLA Ops:
  7.2 0.0 copy-start
  7.2 0.0 all-gather.5.cloned.1.call-start
  7.2 0.7 all-gather.5.cloned.1.call-update
  7.9 0.0 all-gather.3.cloned.1.call-start
  8.0 0.7 all-gather.3.cloned.1.call-update
  8.7 0.0 all-reduce.3.cloned.1.call-start
  8.7 0.7 compare_and_fusion
  9.4 0.1 reshape.41
  9.5 0.7 convert_element_type.12
  10.2 0.0 copy-done
  10.2 3.8 %fusion.10 = f32[4,8,128,128]{3,2,1,0:T(8,128)S(1)} fusion(bf16[4,8,512,128]{3,2,1,0:T(8,128)(2,1)} %param.12, bf16[4,512,128]{2,1,0:T(8,128)(2,1)S(1)} %copy-done), kind=kOutput, calls=%fused_computation.16 | convolution fusion | flops 536870912 | bytes 6815744 | tf_op jit(solution)/shard_map/osnb,ont->osbt/dot_general | solution.py:44
  14.0 15.0 %all-gather.5.cloned.1.call-done = bf16[8,512,128]{2,1,0:T(8,128)(2,1)} async-done(((bf16[2,512,128]{2,1,0:T(8,128)(2,1)}), bf16[8,512,128]{2,1,0:T(8,128)(2,1)}) %all-gather.5.cloned.1.call-update) | async-done | bytes 1048592 | tf_op jit(solution)/shard_map/all_gather | solution.py:36
  29.0 4.3 %gather_fusion.1 = bf16[32,512,128]{2,1,0:T(8,128)(2,1)} fusion(bf16[8,512,128]{2,1,0:T(8,128)(2,1)} %all-gather.5.cloned.1.call-done, s32[1024]{0:T(1024)S(1)} %pad_clamp_fusion), kind=kCustom, calls=%fused_computation.1.clone | custom fusion | bytes 8388736 | tf_op jit(solution)/shard_map/jit(_take)/gather | solution.py:42
  33.3 6.3 %copy.23 = bf16[4,8,512,128]{2,3,1,0:T(8,128)(2,1)} copy(bf16[4,8,512,128]{3,2,1,0:T(8,128)(2,1)} %bitcast.43) | data formatting | bytes 8388608 | tf_op jit(solution)/shard_map/jit(_take)/gather | solution.py:42
  39.7 7.6 %all-gather.3.cloned.1.call-done = bf16[8,512,128]{2,1,0:T(8,128)(2,1)} async-done(((bf16[2,512,128]{2,1,0:T(8,128)(2,1)}), bf16[8,512,128]{2,1,0:T(8,128)(2,1)}) %all-gather.3.cloned.1.call-update) | async-done | bytes 1048592 | tf_op jit(solution)/shard_map/all_gather | solution.py:35
  47.3 4.3 %gather_fusion = bf16[32,512,128]{2,1,0:T(8,128)(2,1)} fusion(bf16[8,512,128]{2,1,0:T(8,128)(2,1)} %all-gather.3.cloned.1.call-done, s32[1024]{0:T(1024)S(1)} %pad_clamp_fusion), kind=kCustom, calls=%fused_computation.clone | custom fusion | bytes 8388736 | tf_op jit(solution)/shard_map/jit(_take)/gather | solution.py:41
  51.6 6.3 %copy.22 = bf16[4,8,512,128]{2,3,1,0:T(8,128)(2,1)} copy(bf16[4,8,512,128]{3,2,1,0:T(8,128)(2,1)} %bitcast.42) | data formatting | bytes 8388608 | tf_op jit(solution)/shard_map/jit(_take)/gather | solution.py:41
  57.8 4.8 %fusion = f32[4,8,128,128]{3,2,1,0:T(8,128)S(1)} fusion(bf16[4,8,512,128]{3,2,1,0:T(8,128)(2,1)} %param.11, bf16[4,8,512,128]{2,3,1,0:T(8,128)(2,1)} %copy.23, pred[4,8]{1,0:T(4,128)(4,1)S(1)} %get-tuple-element.9), kind=kOutput, calls=%fused_computation.2 | convolution fusion | flops 538968064 | bytes 10485792 | tf_op jit(solution)/shard_map/osna,osnb->osab/dot_general | solution.py:43
  62.6 0.0 copy-start.2
  62.6 0.0 copy-start.4
  62.7 2.3 multiply_convert_fusion.1
  65.0 0.6 copy-done.4
  65.6 1.8 fusion.8
  67.4 0.0 copy-done.2
  67.4 1.5 collective-permute-start
  68.9 23.8 %collective-permute-done = f32[4,512,128]{2,1,0:T(8,128)S(1)} collective-permute-done((f32[4,512,128]{2,1,0:T(8,128)S(1)}, f32[4,512,128]{2,1,0:T(8,128)S(1)}, u32[]{:S(2)}, u32[]{:S(2)}) %collective-permute-start) | collective-permute-done | bytes 1048608 | tf_op jit(solution)/shard_map/ppermute | solution.py:16
  92.8 0.2 add.32
  92.9 1.5 collective-permute-start.1
  94.5 22.9 %collective-permute-done.1 = f32[4,512,128]{2,1,0:T(8,128)S(1)} collective-permute-done((f32[4,512,128]{2,1,0:T(8,128)S(1)}, f32[4,512,128]{2,1,0:T(8,128)S(1)}, u32[]{:S(2)}, u32[]{:S(2)}) %collective-permute-start.1) | collective-permute-done | bytes 1048608 | tf_op jit(solution)/shard_map/ppermute | solution.py:16
  117.4 0.1 add.33
  117.5 2.5 collective-permute-start.2
  120.1 44.5 %collective-permute-done.2 = f32[4,512,128]{2,1,0:T(8,128)S(1)} collective-permute-done((f32[4,512,128]{2,1,0:T(8,128)S(1)}, f32[4,512,128]{2,1,0:T(8,128)S(1)}, u32[]{:S(2)}, u32[]{:S(2)}) %collective-permute-start.2) | collective-permute-done | bytes 1048608 | tf_op jit(solution)/shard_map/ppermute | solution.py:16
  164.5 0.1 add.34
  164.6 1.8 fusion.19
  166.5 0.1 copy.27
  166.7 47.1 %custom-call.8 = f32[4,128,128]{2,1,0:T(8,128)S(1)} custom-call(f32[4,128,128]{2,1,0:T(8,128)S(1)} %fusion.15), custom_call_target="Cholesky" | custom-call | tf_op jit(solution)/shard_map/jit(cholesky)/cholesky | solution.py:53
  213.8 0.1 compare_reduce_fusion
  213.9 0.1 select_bitcast_fusion
  214.0 39.5 %custom-call.9 = f32[4,1,128,128]{2,3,1,0:T(8,128)S(1)} custom-call(f32[4,1,128,128]{3,2,1,0:T(8,128)S(1)} %select_bitcast_fusion), custom_call_target="InvertDiagBlocksLowerTriangular" | custom-call | tf_op jit(solution)/shard_map/jit(_solve_triangular)/vmap()/triangular_solve | solution.py:25
  253.5 1.0 fusion.13
  254.6 0.0 copy-start.3
  254.6 3.6 %fusion.3 = f32[4,8,128,128]{3,2,1,0:T(8,128)S(1)} fusion(bf16[4,8,512,128]{2,3,1,0:T(8,128)(2,1)} %copy.22, pred[4,8]{1,0:T(4,128)(4,1)S(1)} %get-tuple-element.9, f32[4,512,128]{2,1,0:T(8,128)S(1)} %fusion.13), kind=kOutput, calls=%fused_computation.6 | convolution fusion | flops 539230208 | bytes 7340064 | tf_op jit(solution)/shard_map/osna,ont->osat/dot_general | solution.py:59
  258.2 0.0 copy-done.3
  258.3 0.0 copy-start.1
  258.3 3.7 %multiply_convert_fusion = bf16[4,8,128,128]{3,2,1,0:T(8,128)(2,1)S(1)} fusion(f32[4,8,128,128]{3,2,1,0:T(8,128)S(1)} %copy-done.3, f32[4,8,128,128]{3,2,1,0:T(8,128)S(1)} %fusion.3, f32[4,8]{1,0:T(4,128)S(1)} %convert_element_type.12), kind=kOutput, calls=%fused_computation.11 | convolution fusion | flops 806354944 | bytes 5243008 | tf_op jit(solution)/shard_map/osab,osat->osbt/dot_general | solution.py:61
  262.0 0.0 copy-done.1
  262.0 0.0 copy-start.5
  262.0 1.5 convolution_bitcast_fusion
  263.6 1.4 copy.31
  264.9 0.0 all-reduce.3.cloned.1.call-update
  264.9 0.0 copy-done.5
  265.0 0.6 dynamic-slice
  266.2 0.7 dynamic-slice_multiply_fusion
  266.9 76.5 %all-reduce.3.cloned.1.call-done = f32[4,512,128]{2,0,1:T(4,128)} async-done(((f32[4,512,128]{2,0,1:T(4,128)}), f32[4,512,128]{2,0,1:T(4,128)}) %all-reduce.3.cloned.1.call-update) | async-done | bytes 1048592
  343.3 0.9 constant_dynamic-slice_fusion
  344.3 0.7 copy.32
  (5 shorter events, 0.1 us)
Async XLA Ops:
  7.2 3.0 copy-start
  7.2 21.8 %all-gather.5.cloned.1.call-start = ((), (), s32[]{:S(2)}) async-start(), calls=%async_computation.1 | async-start | bytes 1310720 | tf_op jit(solution)/shard_map/all_gather | solution.py:36
  7.9 39.4 %all-gather.3.cloned.1.call-start = ((), (), s32[]{:S(2)}) async-start(), calls=%async_computation | async-start | bytes 1310720 | tf_op jit(solution)/shard_map/all_gather | solution.py:35
  8.7 334.7 %all-reduce.3.cloned.1.call-start = ((), (), s32[]{:S(2)}) async-start(), calls=%async_computation.2 | async-start | bytes 2097152
  62.6 4.8 %copy-start.2 = (f32[4,8,128,128]{3,2,1,0:T(8,128)}, f32[4,8,128,128]{3,2,1,0:T(8,128)S(1)}, u32[]{:S(2)}) copy-start(f32[4,8,128,128]{3,2,1,0:T(8,128)S(1)} %fusion) | copy-start | bytes 6291460
  62.6 2.9 copy-start.4
  67.4 25.4 %collective-permute-start = (f32[4,512,128]{2,1,0:T(8,128)S(1)}, f32[4,512,128]{2,1,0:T(8,128)S(1)}, u32[]{:S(2)}, u32[]{:S(2)}) collective-permute-start(f32[4,512,128]{2,1,0:T(8,128)S(1)} %fusion.8), channel_id=1, source_target_pairs={{0,4},{4,0},{8,12},{12,8},{16,20},{20,16},{24,28},{28,24},{1,5},{5... | collective-permute-start | bytes 3145736 | tf_op jit(solution)/shard_map/ppermute | solution.py:16
  92.9 24.5 %collective-permute-start.1 = (f32[4,512,128]{2,1,0:T(8,128)S(1)}, f32[4,512,128]{2,1,0:T(8,128)S(1)}, u32[]{:S(2)}, u32[]{:S(2)}) collective-permute-start(f32[4,512,128]{2,1,0:T(8,128)S(1)} %add.32), channel_id=1, source_target_pairs={{0,8},{4,12},{8,0},{12,4},{16,24},{20,28},{24,16},{28,20},{1,9},{5... | collective-permute-start | bytes 3145736 | tf_op jit(solution)/shard_map/ppermute | solution.py:16
  117.5 47.0 %collective-permute-start.2 = (f32[4,512,128]{2,1,0:T(8,128)S(1)}, f32[4,512,128]{2,1,0:T(8,128)S(1)}, u32[]{:S(2)}, u32[]{:S(2)}) collective-permute-start(f32[4,512,128]{2,1,0:T(8,128)S(1)} %add.33), channel_id=1, source_target_pairs={{0,16},{4,20},{8,24},{12,28},{16,0},{20,4},{24,8},{28,12},{1,17},{... | collective-permute-start | bytes 3145736 | tf_op jit(solution)/shard_map/ppermute | solution.py:16
  254.6 3.7 %copy-start.3 = (f32[4,8,128,128]{3,2,1,0:T(8,128)S(1)}, f32[4,8,128,128]{3,2,1,0:T(8,128)}, u32[]{:S(2)}) copy-start(f32[4,8,128,128]{3,2,1,0:T(8,128)} %copy-done.2) | copy-start | bytes 6291460
  258.3 3.8 %copy-start.1 = (bf16[4,8,512,128]{3,2,1,0:T(8,128)(2,1)S(1)}, bf16[4,8,512,128]{3,2,1,0:T(8,128)(2,1)}, u32[]{:S(2)}) copy-start(bf16[4,8,512,128]{3,2,1,0:T(8,128)(2,1)} %param.12) | copy-start | bytes 12582916
  262.0 2.9 copy-start.5
Sparse Core Ops, SparseCore 0:
  9.5 19.4 all-gather.4
  30.6 16.6 all-gather.2
  265.1 78.2 all-reduce.2
